TPU v7x, 512 devices: a whole 4x4x16 slice. The times are simulated.
512 devices in a mesh: row: 64 (over z, x_hi, core), rep: 8 (over y, x_lo).
Axes of the slice: x: 4 (x_hi: 2, x_lo: 2; x = x_hi * 2 + x_lo), y: 4, z: 16, core: 2. Of those that a mesh axis runs over, the one named last changes fastest.
Arguments:
- features: float32 [65536, 128], P(('row', 'rep')), may hold values from -6 to 6
- weight: float32 [128, 256], replicated, may hold values from -0.5 to 0.5
- bias: float32 [256], replicated, may hold values from -3 to 3
- adjacency: float32 [64, 8, 64, 128, 128], P('row', 'rep')
- tile_row: int32 [64, 8, 64], P('row', 'rep'), may hold values from 0 to 7
- tile_live: int32 [64, 8, 64], P('row', 'rep'), may hold values from 0 to 1
- node_live: int32 [65536], P(('row', 'rep')), may hold values 0 or 1
- cotangent: float32 [65536, 256], P(('row', 'rep'))
Outputs:
- activations: float32 [65536, 256], P(('row', 'rep'))
- weight_grad: float32 [128, 256], replicated
- bias_grad: float32 [256], replicated
All inputs are finite; a program needn't handle non-finite values. No bound on the sum of `node_live` on one device may be relied on, other than what follows from the above.
Results may differ from a plain program's by a relative error of at most 0.0003.
Values sent between devices are 32-bit elements; how exact they have to be, the bound alone decides.
A program may use at most 64 MiB of HBM per device.

v0:
```python
import jax
import jax.numpy as jnp
from jax import lax
from jax.sharding import PartitionSpec as P


def section_terms(adj_tiles, row_slot, live_slot, pieces, totals):
    tile_size = adj_tiles.shape[1]
    piece_rows = pieces[0].shape[0]
    shard_count = piece_rows // tile_size

    def add_tile(k, sums_in):
        tile_now = lax.dynamic_index_in_dim(adj_tiles, k, 0, keepdims=False)
        target = lax.dynamic_index_in_dim(row_slot, k, 0, keepdims=False) * tile_size
        weight_now = lax.dynamic_index_in_dim(live_slot, k, 0, keepdims=False)
        updated = []
        for piece_now, total in zip(pieces, sums_in):
            feat_block = lax.dynamic_slice_in_dim(piece_now, k * tile_size, tile_size, 0)
            tile_term = jnp.dot(tile_now, feat_block, precision=lax.Precision.HIGHEST) * weight_now
            current = lax.dynamic_slice_in_dim(total, target, tile_size, 0)
            updated.append(lax.dynamic_update_slice_in_dim(total, current + tile_term, target, 0))
        return tuple(updated)

    return lax.fori_loop(0, shard_count, add_tile, tuple(totals))


def local(features, weight, bias, adjacency, tile_row, tile_live, node_live, cotangent):
    adj_tiles = adjacency[0, 0]
    row_slot = tile_row[0, 0]
    live_slot = tile_live[0, 0].astype(jnp.float32)
    groups = lax.axis_size("rep")
    tile_size = adj_tiles.shape[1]
    empty_in = jnp.zeros((groups * tile_size, features.shape[1]), jnp.float32)
    partial_in = section_terms(
        adj_tiles,
        row_slot,
        live_slot,
        (lax.all_gather(features, "row", axis=0, tiled=True),),
        (empty_in,),
    )[0]
    aggregated = lax.psum_scatter(partial_in, "rep", scatter_dimension=0, tiled=True)
    projected_sum = jnp.dot(aggregated, weight, precision=lax.Precision.HIGHEST)
    preact = projected_sum + bias
    node_mask = node_live.astype(jnp.float32)[:, None]
    sigmoid_value = jax.nn.sigmoid(preact)
    activations = preact * sigmoid_value * node_mask
    local_grad = cotangent * node_mask * sigmoid_value * (1.0 + preact * (1.0 - sigmoid_value))
    weight_part = lax.dot_general(
        aggregated, local_grad, (((0,), (0,)), ((), ())), precision=lax.Precision.HIGHEST
    )
    bias_part = jnp.sum(local_grad, axis=0)
    weight_grad, bias_grad = lax.psum((weight_part, bias_part), ("row", "rep"))
    return (activations, weight_grad, bias_grad)


def solution(mesh):
    placed = (
        P(("row", "rep"), None),
        P(),
        P(),
        P("row", "rep", None, None, None),
        P("row", "rep", None),
        P("row", "rep", None),
        P(("row", "rep")),
        P(("row", "rep"), None),
    )
    return jax.shard_map(
        local,
        mesh=mesh,
        in_specs=placed,
        out_specs=(P(("row", "rep"), None), P(), P()),
        check_vma=False,
    )
```

profile of v0, /device:TPU:1, one launch (start us, length us, event | category | flops | bytes accessed | tf_op | source)
XLA Modules:
  0.0 943.0 jit_solution(5304687563539046468)
XLA Ops:
  8.6 159.4 %all-gather.2.cloned.1.call-done = f32[8192,128]{1,0:T(8,128)} async-done(((f32[128,128]{1,0:T(8,128)}), f32[8192,128]{1,0:T(8,128)}) %all-gather.2.cloned.1.call-update) | async-done | bytes 4194320 | tf_op jit(solution)/shard_map/all_gather | solution.py:38
  168.1 271.4 %while.13 = (s32[]{:T(128)}, f32[1024,128]{1,0:T(8,128)S(1)}, s32[64]{0:T(128)}, f32[64,128,128]{2,1,0:T(8,128)}, f32[8192,128]{1,0:T(8,128)}, /*index=5*/f32[64...) while((s32[]{:T(128)}, f32[1024,128]{1,0:T(8,128)S(1)}, ...), condition=%wide.region_1.2_spmd, body=%wide.region_0.1_spmd.sunk | while | flops 25198600 | bytes 263409 | solution.py:24
  170.6 1.7 fusion.17
  174.9 1.7 fusion.17
  179.1 1.7 fusion.17
  183.3 1.7 fusion.17
  187.6 1.7 fusion.17
  191.8 1.7 fusion.17
  196.1 1.7 fusion.17
  200.3 1.7 fusion.17
  204.5 1.7 fusion.17
  208.8 1.7 fusion.17
  213.0 1.7 fusion.17
  217.3 1.7 fusion.17
  221.5 1.7 fusion.17
  225.7 1.7 fusion.17
  230.0 1.7 fusion.17
  234.2 1.7 fusion.17
  238.5 1.7 fusion.17
  242.7 1.7 fusion.17
  247.0 1.7 fusion.17
  251.2 1.7 fusion.17
  255.4 1.7 fusion.17
  259.7 1.7 fusion.17
  263.9 1.7 fusion.17
  268.2 1.7 fusion.17
  272.4 1.7 fusion.17
  276.6 1.7 fusion.17
  280.9 1.7 fusion.17
  285.1 1.7 fusion.17
  289.4 1.7 fusion.17
  293.6 1.7 fusion.17
  297.8 1.7 fusion.17
  302.1 1.7 fusion.17
  306.3 1.7 fusion.17
  310.6 1.7 fusion.17
  314.8 1.7 fusion.17
  319.0 1.7 fusion.17
  323.3 1.7 fusion.17
  327.5 1.7 fusion.17
  331.8 1.7 fusion.17
  336.0 1.7 fusion.17
  340.3 1.7 fusion.17
  344.5 1.7 fusion.17
  348.7 1.7 fusion.17
  353.0 1.7 fusion.17
  357.2 1.7 fusion.17
  361.5 1.7 fusion.17
  365.7 1.7 fusion.17
  369.9 1.7 fusion.17
  378.4 1.7 fusion.17
  386.9 1.7 fusion.17
  391.1 1.7 fusion.17
  399.6 1.7 fusion.17
  403.9 1.7 fusion.17
  412.4 1.7 fusion.17
  425.1 1.7 fusion.17
  433.6 1.7 fusion.17
  437.8 1.7 fusion.17
  441.1 34.6 %reduce-scatter.2.cloned.1.call-done = f32[128,128]{1,0:T(8,128)} async-done(((f32[1024,128]{1,0:T(8,128)}), f32[128,128]{1,0:T(8,128)}) %reduce-scatter.2.cloned.1.call-update) | async-done | bytes 65552 | tf_op jit(solution)/shard_map/reduce_scatter | solution.py:41
  475.7 1.9 fusion.6
  477.5 1.8 fusion.7
  479.4 106.9 %psum.15 = f32[256]{0:T(256)} all-reduce(f32[256]{0:T(256)S(1)} %get-tuple-element.125), channel_id=1, replica_groups=mesh['row'=64,'rep'=8] {'row','rep'}, use_global_device_ids=true, to_apply=%region_5.6 | all-reduce | flops 256 | bytes 2048 | tf_op jit(solution)/shard_map/psum | solution.py:52
  586.3 348.6 %all-reduce.2.cloned.1.call-done = f32[128,256]{1,0:T(8,128)} async-done(((f32[128,256]{1,0:T(8,128)}), f32[128,256]{1,0:T(8,128)}) %all-reduce.2.cloned.1.call-update) | async-done | bytes 131088 | tf_op jit(solution)/shard_map/psum | solution.py:52
  (149 shorter events, 133.6 us)
Async XLA Ops:
  7.2 468.5 %copy-start = (f32[128,256]{1,0:T(8,128)S(1)}, f32[128,256]{1,0:T(8,128)}, u32[]{:S(2)}) copy-start(f32[128,256]{1,0:T(8,128)} %param.11) | copy-start | bytes 393220
  7.2 160.9 %all-gather.2.cloned.1.call-start = ((), (), s32[]{:S(2)}) async-start(), calls=%async_computation.1 | async-start | bytes 4259840 | tf_op jit(solution)/shard_map/all_gather | solution.py:38
  7.9 467.7 %reduce-scatter.2.cloned.1.call-start = ((), (), s32[]{:S(2)}) async-start(), calls=%async_computation.2 | async-start | bytes 589824 | tf_op jit(solution)/shard_map/reduce_scatter | solution.py:41
  439.5 0.8 copy-start.1
  440.3 494.6 %all-reduce.2.cloned.1.call-start = ((), (), s32[]{:S(2)}) async-start(), calls=%async_computation.3 | async-start | bytes 262144 | tf_op jit(solution)/shard_map/psum | solution.py:52
Sparse Core Ops, SparseCore 0:
  11.3 156.7 all-gather.1
  440.5 35.1 reduce-scatter.1
  482.6 452.2 all-reduce.1
where the time goes:
time: 948 us; the launch traced here: 943 us
  waiting for transfers between devices  543 us (57%)
  local copies, waits for them, and re-layouts  119 us (13%)
  matrix products  114 us (12%)
  blocking collectives  107 us (11%)
  loops' own time  44.1 us (5%)
  between operations  13.8 us (1%)
    psum x1, waiting for transfers between devices, local(): weight_grad, bias_grad = lax.psum((weight_part, bias_part), ('row', 'rep'))  349 us
    all_gather x1, waiting for transfers between devices, local(): lax.all_gather(features, 'row', axis=0, tiled=True)  159 us
    dot_general x64, matrix products, add_tile(): jnp.dot(tile_now, feat_block, precision=lax.Precision.HIGHEST) * weight_now  110 us
    psum x1, blocking collectives, local(): weight_grad, bias_grad = lax.psum((weight_part, bias_part), ('row', 'rep'))  107 us
    dynamic_slice x64, local copies, waits for them, and re-layouts, add_tile(): lax.dynamic_index_in_dim(row_slot, k, 0, keepdims=False) * tile_size  79.5 us
    another operation x1, loops' own time, section_terms(): return lax.fori_loop(0, shard_count, add_tile, tuple(totals))  44.1 us
    dynamic_slice x64, local copies, waits for them, and re-layouts, add_tile(): weight_now = lax.dynamic_index_in_dim(live_slot, k, 0, keepdims=False)  37.5 us
    reduce_scatter x1, waiting for transfers between devices, local(): lax.psum_scatter(partial_in, 'rep', scatter_dimension=0, tiled=True)  34.6 us
  transfers between devices with their start and end apart: 3, of which 3 were waited for; matrix products, arithmetic and copies ran while one was open for 0% of the time, Pallas kernels for 0%

commit v1 on v0

--- a/solution.py
+++ b/solution.py
@@ -49,7 +49,7 @@
         aggregated, local_grad, (((0,), (0,)), ((), ())), precision=lax.Precision.HIGHEST
     )
     bias_part = jnp.sum(local_grad, axis=0)
-    weight_grad, bias_grad = lax.psum((weight_part, bias_part), ("row", "rep"))
+    weight_grad, bias_grad = lax.psum(lax.psum((weight_part, bias_part), "row"), "rep")
     return (activations, weight_grad, bias_grad)
 
 

time: 948 us -> 1110 us (1.17)
  waiting for transfers between devices: 543 us -> 661 us
  blocking collectives: 107 us -> 145 us
    psum x1 -> x2, waiting for transfers between devices: 349 us -> 466 us  [the longest x1 466 us: local(): lax.psum((weight_part, bias_part), 'row')]
    psum x1 -> x2, blocking collectives: 107 us -> 145 us  [the longest x1 129 us: local(): lax.psum((weight_part, bias_part), 'row')]
  transfers between devices with their start and end apart: 3 -> 4, of which waited for: 3 -> 3; matrix products, arithmetic and copies ran while one was open for 0% -> 0% of each run, Pallas kernels for 0% -> 0%
where the time goes in v1:
time: 1110 us; the launch traced here: 1100 us
  waiting for transfers between devices  661 us (60%)
  blocking collectives  145 us (13%)
  local copies, waits for them, and re-layouts  119 us (11%)
  matrix products  114 us (10%)
  loops' own time  44.1 us (4%)
  between operations  13.8 us (1%)
    psum x1, waiting for transfers between devices, local(): lax.psum((weight_part, bias_part), 'row')  466 us
    all_gather x1, waiting for transfers between devices, local(): lax.all_gather(features, 'row', axis=0, tiled=True)  160 us
    psum x1, blocking collectives, local(): lax.psum((weight_part, bias_part), 'row')  129 us
    dot_general x64, matrix products, add_tile(): jnp.dot(tile_now, feat_block, precision=lax.Precision.HIGHEST) * weight_now  110 us
    dynamic_slice x64, local copies, waits for them, and re-layouts, add_tile(): lax.dynamic_index_in_dim(row_slot, k, 0, keepdims=False) * tile_size  79.5 us
    another operation x1, loops' own time, section_terms(): return lax.fori_loop(0, shard_count, add_tile, tuple(totals))  44.1 us
    dynamic_slice x64, local copies, waits for them, and re-layouts, add_tile(): weight_now = lax.dynamic_index_in_dim(live_slot, k, 0, keepdims=False)  37.5 us
    reduce_scatter x1, waiting for transfers between devices, local(): lax.psum_scatter(partial_in, 'rep', scatter_dimension=0, tiled=True)  34.7 us
  transfers between devices with their start and end apart: 4, of which 3 were waited for; matrix products, arithmetic and copies ran while one was open for 0% of the time, Pallas kernels for 0%

profile of v1, /device:TPU:1, one launch (start us, length us, event | category | flops | bytes accessed | tf_op | source)
XLA Modules:
  0.0 1098.2 jit_solution(1747622113298963911)
XLA Ops:
  8.6 159.5 %all-gather.2.cloned.1.call-done = f32[8192,128]{1,0:T(8,128)} async-done(((f32[128,128]{1,0:T(8,128)}), f32[8192,128]{1,0:T(8,128)}) %all-gather.2.cloned.1.call-update) | async-done | bytes 4194320 | tf_op jit(solution)/shard_map/all_gather | solution.py:38
  168.2 271.4 %while.13 = (s32[]{:T(128)}, f32[1024,128]{1,0:T(8,128)S(1)}, s32[64]{0:T(128)}, f32[64,128,128]{2,1,0:T(8,128)}, f32[8192,128]{1,0:T(8,128)}, /*index=5*/f32[64...) while((s32[]{:T(128)}, f32[1024,128]{1,0:T(8,128)S(1)}, ...), condition=%wide.region_1.2_spmd, body=%wide.region_0.1_spmd.sunk | while | flops 25198600 | bytes 263409 | solution.py:24
  170.7 1.7 fusion.17
  174.9 1.7 fusion.17
  179.2 1.7 fusion.17
  183.4 1.7 fusion.17
  187.6 1.7 fusion.17
  191.9 1.7 fusion.17
  196.1 1.7 fusion.17
  200.4 1.7 fusion.17
  204.6 1.7 fusion.17
  208.8 1.7 fusion.17
  213.1 1.7 fusion.17
  217.3 1.7 fusion.17
  221.6 1.7 fusion.17
  225.8 1.7 fusion.17
  230.1 1.7 fusion.17
  234.3 1.7 fusion.17
  238.5 1.7 fusion.17
  242.8 1.7 fusion.17
  247.0 1.7 fusion.17
  251.3 1.7 fusion.17
  255.5 1.7 fusion.17
  259.7 1.7 fusion.17
  264.0 1.7 fusion.17
  268.2 1.7 fusion.17
  272.5 1.7 fusion.17
  276.7 1.7 fusion.17
  280.9 1.7 fusion.17
  285.2 1.7 fusion.17
  289.4 1.7 fusion.17
  293.7 1.7 fusion.17
  297.9 1.7 fusion.17
  302.2 1.7 fusion.17
  306.4 1.7 fusion.17
  310.6 1.7 fusion.17
  314.9 1.7 fusion.17
  319.1 1.7 fusion.17
  323.4 1.7 fusion.17
  327.6 1.7 fusion.17
  331.8 1.7 fusion.17
  336.1 1.7 fusion.17
  340.3 1.7 fusion.17
  344.6 1.7 fusion.17
  348.8 1.7 fusion.17
  353.0 1.7 fusion.17
  357.3 1.7 fusion.17
  365.8 1.7 fusion.17
  374.2 1.7 fusion.17
  378.5 1.7 fusion.17
  382.7 1.7 fusion.17
  387.0 1.7 fusion.17
  399.7 1.7 fusion.17
  408.2 1.7 fusion.17
  412.4 1.7 fusion.17
  416.7 1.7 fusion.17
  420.9 1.7 fusion.17
  433.6 1.7 fusion.17
  441.1 34.7 %reduce-scatter.2.cloned.1.call-done = f32[128,128]{1,0:T(8,128)} async-done(((f32[1024,128]{1,0:T(8,128)}), f32[128,128]{1,0:T(8,128)}) %reduce-scatter.2.cloned.1.call-update) | async-done | bytes 65552 | tf_op jit(solution)/shard_map/reduce_scatter | solution.py:41
  475.8 1.9 fusion.6
  477.7 1.8 fusion.7
  479.5 465.9 %all-reduce.3.cloned.1.call-done = f32[128,256]{1,0:T(8,128)} async-done(((f32[128,256]{1,0:T(8,128)}), f32[128,256]{1,0:T(8,128)}) %all-reduce.3.cloned.1.call-update) | async-done | bytes 131088 | tf_op jit(solution)/shard_map/psum | solution.py:52
  945.5 128.6 %psum.30 = f32[256]{0:T(256)S(1)} all-reduce(f32[256]{0:T(256)S(1)} %get-tuple-element.125), channel_id=1, replica_groups=mesh['row'=64,'rep'=8] {'row'}, use_global_device_ids=true, to_apply=%region_6.7 | all-reduce | flops 256 | bytes 2048 | tf_op jit(solution)/shard_map/psum | solution.py:52
  1074.0 16.1 %psum.31 = f32[256]{0:T(256)} all-reduce(f32[256]{0:T(256)S(1)} %psum.30), channel_id=1, replica_groups=mesh['row'=64,'rep'=8] {'rep'}, use_global_device_ids=true, to_apply=%region_7.8 | all-reduce | flops 256 | bytes 2048 | tf_op jit(solution)/shard_map/psum | solution.py:52
  (153 shorter events, 135.4 us)
Async XLA Ops:
  7.2 468.6 %copy-start = (f32[128,256]{1,0:T(8,128)S(1)}, f32[128,256]{1,0:T(8,128)}, u32[]{:S(2)}) copy-start(f32[128,256]{1,0:T(8,128)} %param.11) | copy-start | bytes 393220
  7.2 161.0 %all-gather.2.cloned.1.call-start = ((), (), s32[]{:S(2)}) async-start(), calls=%async_computation.1 | async-start | bytes 4259840 | tf_op jit(solution)/shard_map/all_gather | solution.py:38
  7.9 467.9 %reduce-scatter.2.cloned.1.call-start = ((), (), s32[]{:S(2)}) async-start(), calls=%async_computation.2 | async-start | bytes 589824 | tf_op jit(solution)/shard_map/reduce_scatter | solution.py:41
  439.6 0.8 copy-start.1
  440.4 505.0 %all-reduce.3.cloned.1.call-start = ((), (), s32[]{:S(2)}) async-start(), calls=%async_computation.3 | async-start | bytes 262144 | tf_op jit(solution)/shard_map/psum | solution.py:52
  479.5 610.6 %all-reduce.5.cloned.1.call-start = ((), (), s32[]{:S(2)}) async-start(), calls=%async_computation.4 | async-start | bytes 262144 | tf_op jit(solution)/shard_map/psum | solution.py:52
Sparse Core Ops, SparseCore 0:
  11.3 156.7 all-gather.1
  440.5 35.2 reduce-scatter.1
  479.6 465.7 all-reduce.2
  948.2 80.6 all-reduce.4
